TPU v7x, 32 devices: a whole 2x2x4 slice. The times are simulated.
32 devices in a mesh: dp: 8 (over y, x, core), tensor: 4 (over z).
Axes of the slice: x: 2, y: 2, z: 4, core: 2. Of those that a mesh axis runs over, the one named last changes fastest.
Arguments:
- rm_hidden: bfloat16 [8, 256, 3584], P('dp', 'tensor'), may hold values from -6 to 6
- rm_cotangent: bfloat16 [8, 256, 3584], P('dp', 'tensor'), may hold values from -6 to 6
- rm_gain: float32 [3584], replicated, may hold values from 0.25 to 1.75
- rewards: float32 [8], P('dp'), may hold values from 0.25 to 8, as said below
- visual_pos: int32 [8, 128], P('dp', 'tensor'), may hold values from 0 to 255, as said below
- bridge: bfloat16 [3584, 2048], P(None, 'tensor'), may hold values from -0.09375 to 0.09375
- img_query: bfloat16 [8, 512, 2048], P('dp', 'tensor'), may hold values from -8 to 8
- img_key: bfloat16 [8, 512, 2048], P('dp', 'tensor'), may hold values from -8 to 8
- img_value: bfloat16 [8, 512, 2048], P('dp', 'tensor'), may hold values from -6 to 6
Outputs:
- grad_query: bfloat16 [8, 512, 2048], P('dp', 'tensor')
- grad_key: bfloat16 [8, 512, 2048], P('dp', 'tensor')
- grad_value: bfloat16 [8, 512, 2048], P('dp', 'tensor')
Inputs may be any that keep to these rules, and one draw needn't show every extreme that they name: `visual_pos`: strictly increasing in each sample; rows 64 * t to 64 * t + 63 of a reward sequence hold exactly 32 visual tokens, for every t. `rewards`: positive.
All inputs are finite; a program needn't handle non-finite values.
Results may differ from a plain program's by a relative error of at most 0.0082.
Values may be sent and summed in bfloat16 or wider, within the bound.
No kernel may reach another device: no remote copies, remote signals or barrier semaphores. Data moves between devices by JAX's collectives and lax.ppermute only.
A program may use at most 64 MiB of HBM per device.

v0:
```python
import jax
import jax.numpy as jnp
from jax import lax
from jax.sharding import PartitionSpec as P

HD = 128
GW = 64


def norm_backward(hidden, cotangent, gain):
    hidden_f = hidden.astype(jnp.float32)
    scaled_cot = cotangent.astype(jnp.float32) * gain
    inv_rms = lax.rsqrt(jnp.mean(hidden_f * hidden_f, axis=-1, keepdims=True) + 1e-06)
    mixed = jnp.mean(hidden_f * scaled_cot, axis=-1, keepdims=True)
    return (inv_rms * scaled_cot - hidden_f * inv_rms * inv_rms * inv_rms * mixed).astype(
        jnp.bfloat16
    )


def upsample(handed):
    half_width = GW // 2
    grid_rows = handed.reshape(handed.shape[0] // half_width, half_width, handed.shape[1])
    grid_rows = jnp.repeat(jnp.repeat(grid_rows, 2, axis=0), 2, axis=1)
    return grid_rows.reshape(-1, handed.shape[1])


def attend_back(query_rows, key_rows, value_rows, grad_rows):
    seq_length = query_rows.shape[0]
    block_rows = min(512, seq_length)
    score_scale = query_rows.shape[1] ** (-0.5)

    def step(carry, block_index):
        grad_key, grad_value = carry
        first_row = block_index * block_rows
        query_block = lax.dynamic_slice_in_dim(query_rows, first_row, block_rows, 0)
        grad_block = lax.dynamic_slice_in_dim(grad_rows, first_row, block_rows, 0)
        scores = jnp.dot(query_block, key_rows.T, preferred_element_type=jnp.float32) * score_scale
        row_max = jnp.max(scores, axis=1, keepdims=True)
        exp_scores = jnp.exp(scores - row_max)
        attn_weights = exp_scores / jnp.sum(exp_scores, axis=1, keepdims=True)
        weights_half = attn_weights.astype(jnp.bfloat16)
        grad_weights = jnp.dot(grad_block, value_rows.T, preferred_element_type=jnp.float32)
        row_dot = jnp.sum(attn_weights * grad_weights, axis=1, keepdims=True)
        grad_scores = (attn_weights * (grad_weights - row_dot)).astype(jnp.bfloat16)
        grad_query = (
            jnp.dot(grad_scores, key_rows, preferred_element_type=jnp.float32) * score_scale
        ).astype(jnp.bfloat16)
        grad_key = grad_key + jnp.dot(
            grad_scores.T, query_block, preferred_element_type=jnp.float32
        )
        grad_value = grad_value + jnp.dot(
            weights_half.T, grad_block, preferred_element_type=jnp.float32
        )
        return ((grad_key, grad_value), grad_query)

    zeros_init = jnp.zeros(query_rows.shape, jnp.float32)
    carry, query_blocks = lax.scan(
        step, (zeros_init, zeros_init), jnp.arange(seq_length // block_rows, dtype=jnp.int32)
    )
    grad_query = query_blocks.reshape(seq_length, -1)
    grad_key = (carry[0] * score_scale).astype(jnp.bfloat16)
    grad_value = carry[1].astype(jnp.bfloat16)
    return (grad_query, grad_key, grad_value)


def heads_backward(query_rows, key_rows, value_rows, grad_rows):
    seq_length = query_rows.shape[0]
    head_count = query_rows.shape[1] // HD

    def split_heads(array):
        return array.reshape(seq_length, head_count, HD).transpose(1, 0, 2)

    def per_head(head_items):
        return attend_back(head_items[0], head_items[1], head_items[2], head_items[3])

    head_grads = lax.map(
        per_head,
        (
            split_heads(query_rows),
            split_heads(key_rows),
            split_heads(value_rows),
            split_heads(grad_rows),
        ),
    )
    return tuple(
        (grads.transpose(1, 0, 2).reshape(seq_length, head_count * HD) for grads in head_grads)
    )


def local(
    rm_hidden, rm_cotangent, rm_gain, rewards, visual_pos, bridge, img_query, img_key, img_value
):
    reward_sum = lax.psum(jnp.sum(rewards), "dp")
    sample_count = lax.axis_size("dp") * rewards.shape[0]
    reward_weight = rewards[0] * sample_count / reward_sum
    row_offset = lax.axis_index("tensor") * rm_hidden.shape[1]
    local_rows = visual_pos[0] - row_offset
    vis_hidden = jnp.take(rm_hidden[0], local_rows, axis=0)
    vis_cot = jnp.take(rm_cotangent[0], local_rows, axis=0)
    visual_grad = norm_backward(vis_hidden, vis_cot, rm_gain)
    handed = (
        jnp.dot(
            lax.all_gather(visual_grad, "tensor", axis=0, tiled=True),
            bridge,
            preferred_element_type=jnp.float32,
        )
        * reward_weight
    ).astype(jnp.bfloat16)
    grad_rows = upsample(handed)
    head_query, head_key, head_value = (
        lax.all_to_all(img_query[0], "tensor", split_axis=1, concat_axis=0, tiled=True),
        lax.all_to_all(img_key[0], "tensor", split_axis=1, concat_axis=0, tiled=True),
        lax.all_to_all(img_value[0], "tensor", split_axis=1, concat_axis=0, tiled=True),
    )
    head_grads = heads_backward(head_query, head_key, head_value, grad_rows)
    token_query, token_key, token_value = (
        lax.all_to_all(head_grads[0], "tensor", split_axis=0, concat_axis=1, tiled=True),
        lax.all_to_all(head_grads[1], "tensor", split_axis=0, concat_axis=1, tiled=True),
        lax.all_to_all(head_grads[2], "tensor", split_axis=0, concat_axis=1, tiled=True),
    )
    return (token_query[None], token_key[None], token_value[None])


def solution(mesh):
    placed = (
        P("dp", "tensor", None),
        P("dp", "tensor", None),
        P(),
        P("dp"),
        P("dp", "tensor"),
        P(None, "tensor"),
        P("dp", "tensor", None),
        P("dp", "tensor", None),
        P("dp", "tensor", None),
    )
    return jax.shard_map(
        local,
        mesh=mesh,
        in_specs=placed,
        out_specs=(P("dp", "tensor", None), P("dp", "tensor", None), P("dp", "tensor", None)),
        check_vma=False,
    )
```

profile of v0, /device:TPU:2, one launch (start us, length us, event | category | flops | bytes accessed | tf_op | source)
XLA Modules:
  0.0 156.4 jit_solution(5325367002185193584)
XLA Ops:
  0.7 1.5 all_to_all.72
  3.0 4.9 %all-to-all-start = ((bf16[128,4,512]{2,0,1:T(8,128)(2,1)}), bf16[128,4,512]{2,0,1:T(8,128)(2,1)S(1)}, u32[]{:S(2)}, u32[]{:S(2)}) async-start(bf16[128,4,512]{2,0,1:T(8,128)(2,1)} %copy.22), calls=%async_computation | async-start | bytes 1048576 | tf_op jit(solution)/shard_map/all_to_all | solution.py:111
  7.9 1.5 all_to_all.75
  10.3 12.1 %all-to-all-done = bf16[128,4,512]{2,0,1:T(8,128)(2,1)S(1)} async-done(((bf16[128,4,512]{2,0,1:T(8,128)(2,1)}), bf16[128,4,512]{2,0,1:T(8,128)(2,1)S(1)}, u32[]{:S(2)}, u32[]{:S(2)}) %all-to-all-start) | async-done | bytes 524320 | tf_op jit(solution)/shard_map/all_to_all | solution.py:111
  22.4 3.5 %all-to-all-start.1 = ((bf16[128,4,512]{2,0,1:T(8,128)(2,1)}), bf16[128,4,512]{2,0,1:T(8,128)(2,1)S(1)}, u32[]{:S(2)}, u32[]{:S(2)}) async-start(bf16[128,4,512]{2,0,1:T(8,128)(2,1)} %copy.23), calls=%async_computation.1 | async-start | bytes 1048576 | tf_op jit(solution)/shard_map/all_to_all | solution.py:112
  29.0 10.9 %all-to-all-done.1 = bf16[128,4,512]{2,0,1:T(8,128)(2,1)S(1)} async-done(((bf16[128,4,512]{2,0,1:T(8,128)(2,1)}), bf16[128,4,512]{2,0,1:T(8,128)(2,1)S(1)}, u32[]{:S(2)}, u32[]{:S(2)}) %all-to-all-start.1) | async-done | bytes 524320 | tf_op jit(solution)/shard_map/all_to_all | solution.py:112
  39.9 3.5 %all-to-all-start.2 = ((bf16[128,4,512]{2,0,1:T(8,128)(2,1)}), bf16[128,4,512]{2,0,1:T(8,128)(2,1)S(1)}, u32[]{:S(2)}, u32[]{:S(2)}) async-start(bf16[128,4,512]{2,0,1:T(8,128)(2,1)} %copy.24), calls=%async_computation.2 | async-start | bytes 1048576 | tf_op jit(solution)/shard_map/all_to_all | solution.py:113
  44.3 11.3 %psum.7 = f32[]{:T(128)} all-reduce(f32[]{:T(128)} %bitcast.14), channel_id=1, replica_groups=mesh['dp'=8,'tensor'=4] {'dp'}, use_global_device_ids=true, to_apply=%region_2.0 | all-reduce | flops 1 | bytes 8 | tf_op jit(solution)/shard_map/psum | solution.py:93
  56.9 21.2 %all_gather.3 = bf16[128,3584]{1,0:T(8,128)(2,1)S(1)} all-gather(bf16[32,3584]{1,0:T(8,128)(2,1)S(1)} %fusion.38), channel_id=1, replica_groups=mesh['dp'=8,'tensor'=4] {'tensor'}, dimensions={0}, use_global_device_ids=true | all-gather | bytes 1146880 | tf_op jit(solution)/shard_map/all_gather | solution.py:103
  78.1 2.7 %fusion.32 = bf16[128,512]{1,0:T(8,128)(2,1)S(1)} fusion(bf16[128,3584]{1,0:T(8,128)(2,1)S(1)} %all_gather.3, bf16[3584,512]{1,0:T(8,128)(2,1)} %param.18, f32[]{:T(128)S(6)} %div.23), kind=kOutput, calls=%fused_computation.41 | convolution fusion | flops 469893120 | bytes 4718596 | tf_op jit(solution)/shard_map/dot_general | solution.py:102
  83.4 16.3 %while.14 = (s32[]{:T(128)}, bf16[4,512,128]{2,1,0:T(8,128)(2,1)}, bf16[4,512,128]{2,1,0:T(8,128)(2,1)}, bf16[4,512,128]{2,1,0:T(8,128)(2,1)}, bf16[4,512,128]{2...) while((s32[]{:T(128)}, bf16[4,512,128]{2,1,0:T(8,128)(2,1)}, ...), condition=%wide.region_7.9_spmd, body=%wide.region_3.8_spmd.sunk | while | flops 340064768 | bytes 10251357 | solution.py:76
  86.5 1.0 fusion.64
  88.0 1.0 fusion.66
  90.5 1.0 fusion.64
  92.1 1.0 fusion.66
  94.6 1.0 fusion.64
  96.1 1.0 fusion.66
  98.7 1.0 fusion.64
  99.7 1.5 copy.29
  101.2 1.0 all_to_all.81
  102.2 3.8 %all-to-all-start.3 = ((bf16[4,128,512]{2,1,0:T(8,128)(2,1)}), bf16[4,128,512]{2,1,0:T(8,128)(2,1)S(1)}, u32[]{:S(2)}, u32[]{:S(2)}) async-start(bf16[4,128,512]{2,1,0:T(8,128)(2,1)} %all_to_all.81), calls=%async_computation.3 | async-start | bytes 1048576 | tf_op jit(solution)/shard_map/all_to_all | solution.py:117
  106.1 1.4 copy.31
  107.5 1.0 all_to_all.84
  108.5 11.6 %all-to-all-done.3 = bf16[4,128,512]{2,1,0:T(8,128)(2,1)S(1)} async-done(((bf16[4,128,512]{2,1,0:T(8,128)(2,1)}), bf16[4,128,512]{2,1,0:T(8,128)(2,1)S(1)}, u32[]{:S(2)}, u32[]{:S(2)}) %all-to-all-start.3) | async-done | bytes 524320 | tf_op jit(solution)/shard_map/all_to_all | solution.py:117
  120.1 3.5 %all-to-all-start.4 = ((bf16[4,128,512]{2,1,0:T(8,128)(2,1)}), bf16[4,128,512]{2,1,0:T(8,128)(2,1)S(1)}, u32[]{:S(2)}, u32[]{:S(2)}) async-start(bf16[4,128,512]{2,1,0:T(8,128)(2,1)} %all_to_all.84), calls=%async_computation.4 | async-start | bytes 1048576 | tf_op jit(solution)/shard_map/all_to_all | solution.py:118
  124.0 1.0 all_to_all.87
  125.0 12.6 %all-to-all-done.4 = bf16[4,128,512]{2,1,0:T(8,128)(2,1)S(1)} async-done(((bf16[4,128,512]{2,1,0:T(8,128)(2,1)}), bf16[4,128,512]{2,1,0:T(8,128)(2,1)S(1)}, u32[]{:S(2)}, u32[]{:S(2)}) %all-to-all-start.4) | async-done | bytes 524320 | tf_op jit(solution)/shard_map/all_to_all | solution.py:118
  137.6 3.5 %all-to-all-start.5 = ((bf16[4,128,512]{2,1,0:T(8,128)(2,1)}), bf16[4,128,512]{2,1,0:T(8,128)(2,1)S(1)}, u32[]{:S(2)}, u32[]{:S(2)}) async-start(bf16[4,128,512]{2,1,0:T(8,128)(2,1)} %all_to_all.87), calls=%async_computation.5 | async-start | bytes 1048576 | tf_op jit(solution)/shard_map/all_to_all | solution.py:119
  141.4 1.0 copy.35
  142.6 1.0 copy.36
  143.7 11.4 %all-to-all-done.5 = bf16[4,128,512]{2,1,0:T(8,128)(2,1)S(1)} async-done(((bf16[4,128,512]{2,1,0:T(8,128)(2,1)}), bf16[4,128,512]{2,1,0:T(8,128)(2,1)S(1)}, u32[]{:S(2)}, u32[]{:S(2)}) %all-to-all-start.5) | async-done | bytes 524320 | tf_op jit(solution)/shard_map/all_to_all | solution.py:119
  155.4 1.0 copy.37
  (66 shorter events, 18.7 us)
Async XLA Ops:
  0.6 25.3 %copy-start = (bf16[1,64,3584]{2,1,0:T(8,128)(2,1)S(1)}, bf16[1,64,3584]{2,1,0:T(8,128)(2,1)}, u32[]{:S(2)}) copy-start(bf16[1,64,3584]{2,1,0:T(8,128)(2,1)} %param.13) | copy-start | bytes 1376260
  0.6 25.2 %copy-start.7 = (s32[1,32]{1,0:T(1,128)S(1)}, s32[1,32]{1,0:T(1,128)}, u32[]{:S(2)}) copy-start(s32[1,32]{1,0:T(1,128)} %param.17) | copy-start | bytes 388
  2.1 24.5 %copy-start.1 = (bf16[1,64,3584]{2,1,0:T(8,128)(2,1)S(1)}, bf16[1,64,3584]{2,1,0:T(8,128)(2,1)}, u32[]{:S(2)}) copy-start(bf16[1,64,3584]{2,1,0:T(8,128)(2,1)} %param.14) | copy-start | bytes 1376260
  3.0 19.4 %all-to-all-start = ((bf16[128,4,512]{2,0,1:T(8,128)(2,1)}), bf16[128,4,512]{2,0,1:T(8,128)(2,1)S(1)}, u32[]{:S(2)}, u32[]{:S(2)}) async-start(bf16[128,4,512]{2,0,1:T(8,128)(2,1)} %copy.22), calls=%async_computation | async-start | bytes 1048576 | tf_op jit(solution)/shard_map/all_to_all | solution.py:111
  7.9 19.4 %copy-start.2 = (bf16[1,128,2048]{2,1,0:T(8,128)(2,1)S(1)}, bf16[1,128,2048]{2,1,0:T(8,128)(2,1)}, u32[]{:S(2)}) copy-start(bf16[1,128,2048]{2,1,0:T(8,128)(2,1)} %param.21) | copy-start | bytes 1572868
  10.3 18.3 %copy-start.5 = (f32[3584]{0:T(1024)S(1)}, f32[3584]{0:T(1024)}, u32[]{:S(2)}) copy-start(f32[3584]{0:T(1024)} %param.15) | copy-start | bytes 43012
  22.4 17.5 %all-to-all-start.1 = ((bf16[128,4,512]{2,0,1:T(8,128)(2,1)}), bf16[128,4,512]{2,0,1:T(8,128)(2,1)S(1)}, u32[]{:S(2)}, u32[]{:S(2)}) async-start(bf16[128,4,512]{2,0,1:T(8,128)(2,1)} %copy.23), calls=%async_computation.1 | async-start | bytes 1048576 | tf_op jit(solution)/shard_map/all_to_all | solution.py:112
  25.9 14.0 %copy-start.6 = (pred[32]{0:T(512)(128)(4,1)}, pred[32]{0:T(512)(128)(4,1)S(1)}, u32[]{:S(2)}) copy-start(pred[32]{0:T(512)(128)(4,1)S(1)} %get-tuple-element.112) | copy-start | bytes 100
  39.9 42.9 %all-to-all-start.2 = ((bf16[128,4,512]{2,0,1:T(8,128)(2,1)}), bf16[128,4,512]{2,0,1:T(8,128)(2,1)S(1)}, u32[]{:S(2)}, u32[]{:S(2)}) async-start(bf16[128,4,512]{2,0,1:T(8,128)(2,1)} %copy.24), calls=%async_computation.2 | async-start | bytes 1048576 | tf_op jit(solution)/shard_map/all_to_all | solution.py:113
  82.3 1.0 copy-start.3
  99.7 23.9 %copy-start.4 = (bf16[4,512,128]{2,1,0:T(8,128)(2,1)S(1)}, bf16[4,512,128]{2,1,0:T(8,128)(2,1)}, u32[]{:S(2)}) copy-start(bf16[4,512,128]{2,1,0:T(8,128)(2,1)} %get-tuple-element.74) | copy-start | bytes 1572868
  102.2 17.9 %all-to-all-start.3 = ((bf16[4,128,512]{2,1,0:T(8,128)(2,1)}), bf16[4,128,512]{2,1,0:T(8,128)(2,1)S(1)}, u32[]{:S(2)}, u32[]{:S(2)}) async-start(bf16[4,128,512]{2,1,0:T(8,128)(2,1)} %all_to_all.81), calls=%async_computation.3 | async-start | bytes 1048576 | tf_op jit(solution)/shard_map/all_to_all | solution.py:117
  120.1 17.5 %all-to-all-start.4 = ((bf16[4,128,512]{2,1,0:T(8,128)(2,1)}), bf16[4,128,512]{2,1,0:T(8,128)(2,1)S(1)}, u32[]{:S(2)}, u32[]{:S(2)}) async-start(bf16[4,128,512]{2,1,0:T(8,128)(2,1)} %all_to_all.84), calls=%async_computation.4 | async-start | bytes 1048576 | tf_op jit(solution)/shard_map/all_to_all | solution.py:118
  137.6 17.5 %all-to-all-start.5 = ((bf16[4,128,512]{2,1,0:T(8,128)(2,1)}), bf16[4,128,512]{2,1,0:T(8,128)(2,1)S(1)}, u32[]{:S(2)}, u32[]{:S(2)}) async-start(bf16[4,128,512]{2,1,0:T(8,128)(2,1)} %all_to_all.87), calls=%async_computation.5 | async-start | bytes 1048576 | tf_op jit(solution)/shard_map/all_to_all | solution.py:119
where the time goes:
time: 157 us; the launch traced here: 156 us
  waiting for transfers between devices  58.7 us (37%)
  blocking collectives  32.5 us (21%)
  starting transfers between devices  22.6 us (14%)
  local copies, waits for them, and re-layouts  20.1 us (13%)
  matrix products  17 us (11%)
  other arithmetic  3.17 us (2%)
  between operations  2.24 us (1%)
    all_gather x1, blocking collectives, local(): lax.all_gather(visual_grad, 'tensor', axis=0, tiled=True)  21.2 us
    all_to_all x1, waiting for transfers between devices, local(): lax.all_to_all(head_grads[1], 'tensor', split_axis=0, concat_axis=1, tile...  12.6 us
    all_to_all x1, waiting for transfers between devices, local(): lax.all_to_all(img_query[0], 'tensor', split_axis=1, concat_axis=0, tiled...  12.1 us
    all_to_all x1, waiting for transfers between devices, local(): lax.all_to_all(head_grads[0], 'tensor', split_axis=0, concat_axis=1, tile...  11.6 us
    all_to_all x1, waiting for transfers between devices, local(): lax.all_to_all(head_grads[2], 'tensor', split_axis=0, concat_axis=1, tile...  11.4 us
    psum x1, blocking collectives, local(): reward_sum = lax.psum(jnp.sum(rewards), 'dp')  11.3 us
    all_to_all x1, waiting for transfers between devices, local(): lax.all_to_all(img_key[0], 'tensor', split_axis=1, concat_axis=0, tiled=T...  10.9 us
    all_to_all x1, starting transfers between devices, local(): lax.all_to_all(img_query[0], 'tensor', split_axis=1, concat_axis=0, tiled...  4.87 us
  transfers between devices with their start and end apart: 6, of which 5 were waited for; matrix products, arithmetic and copies ran while one was open for 9% of the time, Pallas kernels for 0%

commit v1 on v0

--- a/solution.py
+++ b/solution.py
@@ -113,8 +113,15 @@
         lax.all_to_all(img_value[0], "tensor", split_axis=1, concat_axis=0, tiled=True),
     )
     head_grads = heads_backward(head_query, head_key, head_value, grad_rows)
+
+    def targets_recast(view, axis_id):
+        w_next = lax.all_to_all(
+            jnp.stack(jnp.split(view, lax.axis_size(axis_id), axis=0)), axis_id, 0, 0
+        )
+        return jnp.concatenate(w_next, axis=1)
+
     token_query, token_key, token_value = (
-        lax.all_to_all(head_grads[0], "tensor", split_axis=0, concat_axis=1, tiled=True),
+        targets_recast(head_grads[0], "tensor"),
         lax.all_to_all(head_grads[1], "tensor", split_axis=0, concat_axis=1, tiled=True),
         lax.all_to_all(head_grads[2], "tensor", split_axis=0, concat_axis=1, tiled=True),
     )

time: 157 us -> 161 us (1.025)
  local copies, waits for them, and re-layouts: 20.1 us -> 22 us
    dot_general x4, matrix products: 1.31 us -> 4.91 us  [step(): jnp.dot(grad_block, value_rows.T, preferred_element_type=jnp.float32)]
    dynamic_update_slice x0 -> x8, local copies, waits for them, and re-layouts: none -> 3.14 us  [heads_backward(): lax.map(per_head, (split_heads(query_rows), split_heads(key_rows), split_...]
    dot_general x4, matrix products: 4.04 us -> 1.4 us  [step(): jnp.dot(grad_scores, key_rows, preferred_element_type=jnp.float32)]
    transpose x3 -> x2, local copies, waits for them, and re-layouts: 3.36 us -> 1.86 us  [heads_backward(): grads.transpose(1, 0, 2).reshape(seq_length, head_count * HD)]
  transfers between devices with their start and end apart: 6 -> 6, of which waited for: 5 -> 5; matrix products, arithmetic and copies ran while one was open for 9% -> 8% of each run, Pallas kernels for 0% -> 0%
where the time goes in v1:
time: 161 us; the launch traced here: 160 us
  waiting for transfers between devices  59 us (37%)
  blocking collectives  32.5 us (20%)
  starting transfers between devices  22.6 us (14%)
  local copies, waits for them, and re-layouts  22 us (14%)
  matrix products  18 us (11%)
  other arithmetic  4.04 us (3%)
  between operations  2.25 us (1%)
    all_gather x1, blocking collectives, local(): lax.all_gather(visual_grad, 'tensor', axis=0, tiled=True)  21.2 us
    all_to_all x1, waiting for transfers between devices, local(): lax.all_to_all(head_grads[1], 'tensor', split_axis=0, concat_axis=1, tile...  12.6 us
    all_to_all x1, waiting for transfers between devices, local(): lax.all_to_all(img_query[0], 'tensor', split_axis=1, concat_axis=0, tiled...  12.1 us
    all_to_all x1, waiting for transfers between devices, local(): lax.all_to_all(head_grads[2], 'tensor', split_axis=0, concat_axis=1, tile...  11.7 us
    all_to_all x1, waiting for transfers between devices, targets_recast(): lax.all_to_all(jnp.stack(jnp.split(view, lax.axis_size(axis_id), axis=0))...  11.6 us
    psum x1, blocking collectives, local(): reward_sum = lax.psum(jnp.sum(rewards), 'dp')  11.3 us
    all_to_all x1, waiting for transfers between devices, local(): lax.all_to_all(img_key[0], 'tensor', split_axis=1, concat_axis=0, tiled=T...  10.9 us
    dot_general x4, matrix products, step(): jnp.dot(grad_block, value_rows.T, preferred_element_type=jnp.float32)  4.91 us
  transfers between devices with their start and end apart: 6, of which 5 were waited for; matrix products, arithmetic and copies ran while one was open for 8% of the time, Pallas kernels for 0%

profile of v1, /device:TPU:2, one launch (start us, length us, event | category | flops | bytes accessed | tf_op | source)
XLA Modules:
  0.0 160.5 jit_solution(3399656943508742722)
XLA Ops:
  0.7 1.5 all_to_all.63
  3.0 4.9 %all-to-all-start = ((bf16[128,4,512]{2,0,1:T(8,128)(2,1)}), bf16[128,4,512]{2,0,1:T(8,128)(2,1)S(1)}, u32[]{:S(2)}, u32[]{:S(2)}) async-start(bf16[128,4,512]{2,0,1:T(8,128)(2,1)} %copy.23), calls=%async_computation | async-start | bytes 1048576 | tf_op jit(solution)/shard_map/all_to_all | solution.py:111
  7.9 1.5 all_to_all.66
  10.3 12.1 %all-to-all-done = bf16[128,4,512]{2,0,1:T(8,128)(2,1)S(1)} async-done(((bf16[128,4,512]{2,0,1:T(8,128)(2,1)}), bf16[128,4,512]{2,0,1:T(8,128)(2,1)S(1)}, u32[]{:S(2)}, u32[]{:S(2)}) %all-to-all-start) | async-done | bytes 524320 | tf_op jit(solution)/shard_map/all_to_all | solution.py:111
  22.4 3.5 %all-to-all-start.1 = ((bf16[128,4,512]{2,0,1:T(8,128)(2,1)}), bf16[128,4,512]{2,0,1:T(8,128)(2,1)S(1)}, u32[]{:S(2)}, u32[]{:S(2)}) async-start(bf16[128,4,512]{2,0,1:T(8,128)(2,1)} %copy.24), calls=%async_computation.1 | async-start | bytes 1048576 | tf_op jit(solution)/shard_map/all_to_all | solution.py:112
  29.0 10.9 %all-to-all-done.1 = bf16[128,4,512]{2,0,1:T(8,128)(2,1)S(1)} async-done(((bf16[128,4,512]{2,0,1:T(8,128)(2,1)}), bf16[128,4,512]{2,0,1:T(8,128)(2,1)S(1)}, u32[]{:S(2)}, u32[]{:S(2)}) %all-to-all-start.1) | async-done | bytes 524320 | tf_op jit(solution)/shard_map/all_to_all | solution.py:112
  39.9 3.5 %all-to-all-start.2 = ((bf16[128,4,512]{2,0,1:T(8,128)(2,1)}), bf16[128,4,512]{2,0,1:T(8,128)(2,1)S(1)}, u32[]{:S(2)}, u32[]{:S(2)}) async-start(bf16[128,4,512]{2,0,1:T(8,128)(2,1)} %copy.25), calls=%async_computation.2 | async-start | bytes 1048576 | tf_op jit(solution)/shard_map/all_to_all | solution.py:113
  44.3 11.3 %psum.7 = f32[]{:T(128)} all-reduce(f32[]{:T(128)} %bitcast.14), channel_id=1, replica_groups=mesh['dp'=8,'tensor'=4] {'dp'}, use_global_device_ids=true, to_apply=%region_2.0 | all-reduce | flops 1 | bytes 8 | tf_op jit(solution)/shard_map/psum | solution.py:93
  56.9 21.2 %all_gather.3 = bf16[128,3584]{1,0:T(8,128)(2,1)S(1)} all-gather(bf16[32,3584]{1,0:T(8,128)(2,1)S(1)} %fusion.37), channel_id=1, replica_groups=mesh['dp'=8,'tensor'=4] {'tensor'}, dimensions={0}, use_global_device_ids=true | all-gather | bytes 1146880 | tf_op jit(solution)/shard_map/all_gather | solution.py:103
  78.1 2.7 %fusion.31 = bf16[128,512]{1,0:T(8,128)(2,1)S(1)} fusion(bf16[128,3584]{1,0:T(8,128)(2,1)S(1)} %all_gather.3, bf16[3584,512]{1,0:T(8,128)(2,1)} %param.18, f32[]{:T(128)S(6)} %div.23), kind=kOutput, calls=%fused_computation.41 | convolution fusion | flops 469893120 | bytes 4718596 | tf_op jit(solution)/shard_map/dot_general | solution.py:102
  83.7 20.4 %while.14 = (s32[]{:T(128)}, bf16[4,512,128]{1,2,0:T(8,128)(2,1)}, bf16[4,512,128]{2,1,0:T(8,128)(2,1)}, bf16[4,512,128]{2,1,0:T(8,128)(2,1)}, bf16[4,512,128]{2...) while((s32[]{:T(128)}, bf16[4,512,128]{1,2,0:T(8,128)(2,1)}, ...), condition=%wide.region_7.9_spmd, body=%wide.region_3.8_spmd.sunk | while | flops 340064768 | bytes 10775137 | solution.py:76
  84.2 1.0 fusion.66
  85.2 1.2 multiply_reduce_fusion.2
  89.4 1.0 fusion.66
  90.4 1.2 multiply_reduce_fusion.2
  94.5 1.0 fusion.66
  95.5 1.2 multiply_reduce_fusion.2
  99.6 1.0 fusion.66
  100.6 1.2 multiply_reduce_fusion.2
  104.2 1.2 fusion.40
  106.3 3.9 %all-to-all-start.3 = ((bf16[4,128,512]{1,2,0:T(8,128)(2,1)}), bf16[4,128,512]{1,2,0:T(8,128)(2,1)S(1)}, u32[]{:S(2)}, u32[]{:S(2)}) async-start(bf16[4,128,512]{1,2,0:T(8,128)(2,1)} %pad_maximum_fusion), calls=%async_computation.3 | async-start | bytes 1048576 | tf_op jit(solution)/shard_map/all_to_all | solution.py:118
  110.1 1.4 copy.31
  111.6 1.0 all_to_all.73
  112.6 11.6 %all-to-all-done.3 = bf16[4,128,512]{1,2,0:T(8,128)(2,1)S(1)} async-done(((bf16[4,128,512]{1,2,0:T(8,128)(2,1)}), bf16[4,128,512]{1,2,0:T(8,128)(2,1)S(1)}, u32[]{:S(2)}, u32[]{:S(2)}) %all-to-all-start.3) | async-done | bytes 524320 | tf_op jit(solution)/shard_map/all_to_all | solution.py:118
  124.2 3.5 %all-to-all-start.4 = ((bf16[4,128,512]{2,1,0:T(8,128)(2,1)}), bf16[4,128,512]{2,1,0:T(8,128)(2,1)S(1)}, u32[]{:S(2)}, u32[]{:S(2)}) async-start(bf16[4,128,512]{2,1,0:T(8,128)(2,1)} %all_to_all.73), calls=%async_computation.4 | async-start | bytes 1048576 | tf_op jit(solution)/shard_map/all_to_all | solution.py:125
  128.1 1.0 all_to_all.76
  129.1 12.6 %all-to-all-done.4 = bf16[4,128,512]{2,1,0:T(8,128)(2,1)S(1)} async-done(((bf16[4,128,512]{2,1,0:T(8,128)(2,1)}), bf16[4,128,512]{2,1,0:T(8,128)(2,1)S(1)}, u32[]{:S(2)}, u32[]{:S(2)}) %all-to-all-start.4) | async-done | bytes 524320 | tf_op jit(solution)/shard_map/all_to_all | solution.py:125
  141.7 3.5 %all-to-all-start.5 = ((bf16[4,128,512]{2,1,0:T(8,128)(2,1)}), bf16[4,128,512]{2,1,0:T(8,128)(2,1)S(1)}, u32[]{:S(2)}, u32[]{:S(2)}) async-start(bf16[4,128,512]{2,1,0:T(8,128)(2,1)} %all_to_all.76), calls=%async_computation.5 | async-start | bytes 1048576 | tf_op jit(solution)/shard_map/all_to_all | solution.py:126
  145.2 1.0 copy.35
  146.4 1.0 copy.36
  147.4 11.7 %all-to-all-done.5 = bf16[4,128,512]{2,1,0:T(8,128)(2,1)S(1)} async-done(((bf16[4,128,512]{2,1,0:T(8,128)(2,1)}), bf16[4,128,512]{2,1,0:T(8,128)(2,1)S(1)}, u32[]{:S(2)}, u32[]{:S(2)}) %all-to-all-start.5) | async-done | bytes 524320 | tf_op jit(solution)/shard_map/all_to_all | solution.py:126
  159.4 1.0 copy.37
  (73 shorter events, 21.9 us)
Async XLA Ops:
  0.6 25.3 %copy-start = (bf16[1,64,3584]{2,1,0:T(8,128)(2,1)S(1)}, bf16[1,64,3584]{2,1,0:T(8,128)(2,1)}, u32[]{:S(2)}) copy-start(bf16[1,64,3584]{2,1,0:T(8,128)(2,1)} %param.13) | copy-start | bytes 1376260
  0.6 25.2 %copy-start.7 = (s32[1,32]{1,0:T(1,128)S(1)}, s32[1,32]{1,0:T(1,128)}, u32[]{:S(2)}) copy-start(s32[1,32]{1,0:T(1,128)} %param.17) | copy-start | bytes 388
  2.1 24.5 %copy-start.1 = (bf16[1,64,3584]{2,1,0:T(8,128)(2,1)S(1)}, bf16[1,64,3584]{2,1,0:T(8,128)(2,1)}, u32[]{:S(2)}) copy-start(bf16[1,64,3584]{2,1,0:T(8,128)(2,1)} %param.14) | copy-start | bytes 1376260
  3.0 19.4 %all-to-all-start = ((bf16[128,4,512]{2,0,1:T(8,128)(2,1)}), bf16[128,4,512]{2,0,1:T(8,128)(2,1)S(1)}, u32[]{:S(2)}, u32[]{:S(2)}) async-start(bf16[128,4,512]{2,0,1:T(8,128)(2,1)} %copy.23), calls=%async_computation | async-start | bytes 1048576 | tf_op jit(solution)/shard_map/all_to_all | solution.py:111
  7.9 19.4 %copy-start.2 = (bf16[1,128,2048]{2,1,0:T(8,128)(2,1)S(1)}, bf16[1,128,2048]{2,1,0:T(8,128)(2,1)}, u32[]{:S(2)}) copy-start(bf16[1,128,2048]{2,1,0:T(8,128)(2,1)} %param.21) | copy-start | bytes 1572868
  10.3 18.3 %copy-start.5 = (f32[3584]{0:T(1024)S(1)}, f32[3584]{0:T(1024)}, u32[]{:S(2)}) copy-start(f32[3584]{0:T(1024)} %param.15) | copy-start | bytes 43012
  22.4 17.5 %all-to-all-start.1 = ((bf16[128,4,512]{2,0,1:T(8,128)(2,1)}), bf16[128,4,512]{2,0,1:T(8,128)(2,1)S(1)}, u32[]{:S(2)}, u32[]{:S(2)}) async-start(bf16[128,4,512]{2,0,1:T(8,128)(2,1)} %copy.24), calls=%async_computation.1 | async-start | bytes 1048576 | tf_op jit(solution)/shard_map/all_to_all | solution.py:112
  25.9 14.0 %copy-start.6 = (pred[32]{0:T(512)(128)(4,1)}, pred[32]{0:T(512)(128)(4,1)S(1)}, u32[]{:S(2)}) copy-start(pred[32]{0:T(512)(128)(4,1)S(1)} %get-tuple-element.115) | copy-start | bytes 100
  39.9 42.8 %all-to-all-start.2 = ((bf16[128,4,512]{2,0,1:T(8,128)(2,1)}), bf16[128,4,512]{2,0,1:T(8,128)(2,1)S(1)}, u32[]{:S(2)}, u32[]{:S(2)}) async-start(bf16[128,4,512]{2,0,1:T(8,128)(2,1)} %copy.25), calls=%async_computation.2 | async-start | bytes 1048576 | tf_op jit(solution)/shard_map/all_to_all | solution.py:113
  82.3 1.4 copy-start.3
  104.2 23.5 %copy-start.4 = (bf16[4,512,128]{2,1,0:T(8,128)(2,1)S(1)}, bf16[4,512,128]{2,1,0:T(8,128)(2,1)}, u32[]{:S(2)}) copy-start(bf16[4,512,128]{2,1,0:T(8,128)(2,1)} %get-tuple-element.74) | copy-start | bytes 1572868
  106.3 17.9 %all-to-all-start.3 = ((bf16[4,128,512]{1,2,0:T(8,128)(2,1)}), bf16[4,128,512]{1,2,0:T(8,128)(2,1)S(1)}, u32[]{:S(2)}, u32[]{:S(2)}) async-start(bf16[4,128,512]{1,2,0:T(8,128)(2,1)} %pad_maximum_fusion), calls=%async_computation.3 | async-start | bytes 1048576 | tf_op jit(solution)/shard_map/all_to_all | solution.py:118
  124.2 17.5 %all-to-all-start.4 = ((bf16[4,128,512]{2,1,0:T(8,128)(2,1)}), bf16[4,128,512]{2,1,0:T(8,128)(2,1)S(1)}, u32[]{:S(2)}, u32[]{:S(2)}) async-start(bf16[4,128,512]{2,1,0:T(8,128)(2,1)} %all_to_all.73), calls=%async_computation.4 | async-start | bytes 1048576 | tf_op jit(solution)/shard_map/all_to_all | solution.py:125
  141.7 17.5 %all-to-all-start.5 = ((bf16[4,128,512]{2,1,0:T(8,128)(2,1)}), bf16[4,128,512]{2,1,0:T(8,128)(2,1)S(1)}, u32[]{:S(2)}, u32[]{:S(2)}) async-start(bf16[4,128,512]{2,1,0:T(8,128)(2,1)} %all_to_all.76), calls=%async_computation.5 | async-start | bytes 1048576 | tf_op jit(solution)/shard_map/all_to_all | solution.py:126
